TPU v7x, 32 devices: a whole 2x2x4 slice. The times are simulated.
32 devices in a mesh: ens: 2 (over y), lon: 4 (over z), dom: 4 (over x, core).
Axes of the slice: x: 2, y: 2, z: 4, core: 2. Of those that a mesh axis runs over, the one named last changes fastest.
Arguments:
- particles: bfloat16 [16, 69, 96, 256], P(('ens', 'dom'), None, 'lon'), parts along dimension 0, may hold values from -6 to 6
- observed: bfloat16 [138, 96, 256], P('ens', 'lon'), parts along dimension 0, may hold values from -6 to 6
- precision: float32 [192, 256], P(('ens', 'lon')), parts along dimension 0, may hold values from 0.25 to 12, as said below
- stations: int32 [192, 256], P(('ens', 'lon')), parts along dimension 0, may hold values 0 or 1
- ancestors: int32 [16], P(('ens', 'dom')), parts along dimension 0, may hold values from 0 to 7
- tempering: float32 [2], P('ens'), parts along dimension 0, may hold values from 1 to 4
- w_in: bfloat16 [3, 3, 64, 69], replicated, may hold values from -0.25 to 0.25
- w_mid: bfloat16 [3, 3, 64, 64], replicated, may hold values from -0.25 to 0.25
- w_out: bfloat16 [3, 3, 69, 64], replicated, may hold values from -0.25 to 0.25
Outputs:
- new_particles: bfloat16 [16, 69, 96, 256], P(('ens', 'dom'), None, 'lon'), parts along dimension 0
- weights: float32 [16], P(('ens', 'dom')), parts along dimension 0
There are 2 independent parts, one for each index of `ens`. A program takes and returns all parts, laid end to end along the dimension named above; an argument that names none is the same for every part. Nothing has to cross between parts.
Inputs may be any that keep to these rules, and one draw needn't show every extreme that they name: `precision`: positive everywhere; no other structure is promised. Slot s continues particle ancestors[s]; a particle may be continued by several slots or by none.
All inputs are finite; a program needn't handle non-finite values. No bound on the sum of `stations` on one device may be relied on, other than what follows from the above.
Results may differ from a plain program's by a relative error of at most 0.0021.
Values may be sent and summed in bfloat16 or wider, within the bound.
A program may use at most 128 MiB of HBM per device.

v0:
```python
import jax
import jax.numpy as jnp
from jax import lax
from jax.sharding import PartitionSpec as P


def extended_2(block, sides, width):
    for axis, dim in sides:
        count = lax.axis_size(axis)
        forward = [(i, i + 1) for i in range(count - 1)]
        forward.append((count - 1, 0))
        backward = [(target, source) for source, target in forward]
        low = lax.ppermute(
            lax.slice_in_dim(block, block.shape[dim] - width, None, axis=dim), axis, forward
        )
        high = lax.ppermute(lax.slice_in_dim(block, 0, width, axis=dim), axis, backward)
        block = jnp.concatenate([low, block, high], axis=dim)
    return block


def conv_local(extended, weight):
    out_width = extended.shape[2] - 2
    lat_rows = extended.shape[3]
    padded = jnp.pad(extended, ((0, 0), (0, 0), (0, 0), (1, 1)))
    summed = jnp.zeros((extended.shape[0], weight.shape[2], out_width, lat_rows), jnp.float32)
    for row_tap in range(3):
        for col_tap in range(3):
            window = padded[:, :, row_tap : row_tap + out_width, col_tap : col_tap + lat_rows]
            summed = summed + jnp.einsum(
                "oc,pcxy->poxy",
                weight[row_tap, col_tap],
                window,
                preferred_element_type=jnp.float32,
            )
    return summed


def denoise_local(states, observed, obs_weight, w_in, w_mid, w_out):
    extended = extended_2(states, (("lon", 2),), 1)
    first_act = jax.nn.silu(conv_local(extended, w_in)).astype(jnp.bfloat16)
    first_ext = extended_2(first_act, (("lon", 2),), 1)
    second_act = jax.nn.silu(conv_local(first_ext, w_mid)).astype(jnp.bfloat16)
    second_ext = extended_2(second_act, (("lon", 2),), 1)
    noise_pred = conv_local(second_ext, w_out)
    current = states.astype(jnp.float32)
    updated = (
        current
        - 0.5 * noise_pred
        + 0.25 * obs_weight[None, None] * (observed.astype(jnp.float32)[None] - current)
    )
    return updated.astype(jnp.bfloat16)


def continue_slots(slabs, slot_ancestors):
    slab_piece = lax.all_gather(slabs, "dom", axis=0, tiled=True)
    piece_rows = slab_piece.shape[0]
    inside = (slot_ancestors >= 0) & (slot_ancestors < piece_rows)
    chosen = jnp.take(slab_piece, jnp.clip(slot_ancestors, 0, piece_rows - 1), axis=0)
    return jnp.where(inside[:, None, None, None], chosen, jnp.zeros_like(slabs))


def on_device(particles, observed, precision, stations, ancestors, tempering, w_in, w_mid, w_out):
    obs_weight = stations.astype(jnp.float32) * precision
    misfit_cell = particles.astype(jnp.float32) - observed.astype(jnp.float32)[None]
    local_sums = jnp.sum(obs_weight[None, None] * misfit_cell * misfit_cell, axis=(1, 2, 3))
    band_sums = lax.psum(local_sums, "lon")
    every_sum = lax.all_gather(band_sums, "dom", axis=0, tiled=True)
    center = jnp.mean(every_sum)
    deviation = every_sum - center
    spread = jnp.sqrt(jnp.mean(deviation * deviation) + 1.0)
    log_weights = -0.5 * tempering[0] * deviation / spread
    expo = jnp.exp(log_weights)
    weights_all = expo / jnp.sum(expo)
    slot_count = ancestors.shape[0]
    own_weights = lax.dynamic_slice_in_dim(
        weights_all, lax.axis_index("dom") * slot_count, slot_count
    )
    continued = continue_slots(particles, ancestors)
    new_particles = denoise_local(continued, observed, obs_weight, w_in, w_mid, w_out)
    return (new_particles, own_weights)


def solution(mesh):
    return jax.shard_map(
        on_device,
        mesh=mesh,
        in_specs=(
            P(("ens", "dom"), None, "lon", None),
            P("ens", "lon", None),
            P(("ens", "lon"), None),
            P(("ens", "lon"), None),
            P(("ens", "dom")),
            P("ens"),
            P(),
            P(),
            P(),
        ),
        out_specs=(P(("ens", "dom"), None, "lon", None), P(("ens", "dom"))),
        check_vma=False,
    )
```

profile of v0, /device:TPU:0, one launch (start us, length us, event | category | flops | bytes accessed | tf_op | source)
XLA Modules:
  0.0 159.0 jit_solution(17750243368687318687)
XLA Ops:
  10.2 13.4 %psum.7 = f32[2]{0:T(128)S(1)} all-reduce(f32[2]{0:T(128)S(1)} %fusion.5), channel_id=1, replica_groups=mesh['ens'=2,'lon'=4,'dom'=4] {'lon'}, use_global_device_ids=true, to_apply=%region_1.0 | all-reduce | flops 2 | bytes 16 | tf_op jit(solution)/shard_map/psum | solution.py:66
  25.1 6.1 %all-reduce.3 = f32[8]{0:T(128)S(1)} all-reduce(f32[8]{0:T(128)S(1)} %dynamic-update-slice), channel_id=1, replica_groups=mesh['ens'=2,'lon'=4,'dom'=4] {'dom'}, use_global_device_ids=true, to_apply=%add.3 | all-reduce | flops 8 | bytes 64
  36.4 25.2 %all-gather.2.cloned.1.call-done = bf16[8,69,24,256]{3,2,1,0:T(8,128)(2,1)} async-done(((bf16[2,69,24,256]{3,2,1,0:T(8,128)(2,1)}), bf16[8,69,24,256]{3,2,1,0:T(8,128)(2,1)}) %all-gather.2.cloned.1.call-update) | async-done | bytes 6782992 | tf_op jit(solution)/shard_map/all_gather | solution.py:55
  61.6 3.6 %gather_fusion = bf16[2,69,24,256]{3,2,1,0:T(8,128)(2,1)S(1)} fusion(bf16[8,69,24,256]{3,2,1,0:T(8,128)(2,1)} %all-gather.2.cloned.1.call-done, s32[1024]{0:T(1024)S(1)} %pad_clamp_fusion), kind=kCustom, calls=%fused_computation | custom fusion | bytes 3391496 | tf_op jit(solution)/shard_map/jit(_take)/gather | solution.py:58
  67.2 2.3 %collective-permute-start.1 = (bf16[2,69,1,256]{3,1,2,0:T(8,128)(2,1)S(1)}, bf16[2,69,1,256]{3,1,2,0:T(8,128)(2,1)S(1)}, u32[]{:S(2)}, u32[]{:S(2)}) collective-permute-start(bf16[2,69,1,256]{3,1,2,0:T(8,128)(2,1)S(1)} %get-tuple-element.15), channel_id=1, source_target_pairs={{4,0},{8,4},{12,8},{0,12},{5,1},{9,5},{13,9},{1,13},{6,2},{10,6},{... | collective-permute-start | bytes 211976 | tf_op jit(solution)/shard_map/ppermute | solution.py:16
  69.6 2.6 %fusion.111 = f32[2,24,256,64]{2,3,1,0:T(8,128)} fusion(bf16[3,3,64,69]{3,2,1,0:T(8,128)(2,1)S(1)} %copy-done.3, bf16[2,69,24,256]{3,2,1,0:T(8,128)(2,1)S(1)} %gather_fusion, pred[2]{0:T(512)(128)(4,1)S(1)} %get-tuple-element.12, pred[2]{0:T(512)(128)(4,1)S(1)} %get-tuple-element.20), kind=kOutput, calls=%fused_computation.123 | convolution fusion | flops 110223360 | bytes 4858880 | tf_op jit(solution)/shard_map/oc,pcxy->poxy/dot_general | solution.py:29
  77.8 2.2 %fusion.42 = f32[2,24,256,64]{2,3,1,0:T(8,128)} fusion(bf16[2,69,26,258]{3,1,2,0:T(8,128)(2,1)S(1)} %fusion.18, bf16[3,3,64,69]{3,2,1,0:T(8,128)(2,1)S(1)} %copy-done.3), kind=kOutput, calls=%fused_computation.56 | convolution fusion | flops 108527616 | bytes 4931584 | tf_op jit(solution)/shard_map/oc,pcxy->poxy/dot_general | solution.py:29
  80.0 2.2 %fusion.24 = f32[2,24,256,64]{2,3,1,0:T(8,128)} fusion(bf16[2,69,24,256]{3,1,2,0:T(8,128)(2,1)S(1)} %fusion.44, bf16[2,69,1,256]{3,1,2,0:T(8,128)(2,1)S(1)} %collective-permute-done, bf16[3,3,64,69]{3,2,1,0:T(8,128)(2,1)S(1)} %copy-done.3), kind=kOutput, calls=%fused_computation.38 | convolution fusion | flops 112060416 | bytes 5005312 | tf_op jit(solution)/shard_map/oc,pcxy->poxy/dot_general | solution.py:29
  82.2 2.2 %fusion.28 = f32[2,24,256,64]{2,3,1,0:T(8,128)} fusion(bf16[2,69,1,256]{3,1,2,0:T(8,128)(2,1)S(1)} %collective-permute-done.1, bf16[2,69,24,256]{3,1,2,0:T(8,128)(2,1)S(1)} %fusion.44, bf16[3,3,64,69]{3,2,1,0:T(8,128)(2,1)S(1)} %copy-done.3), kind=kOutput, calls=%fused_computation.42 | convolution fusion | flops 112060416 | bytes 5005312 | tf_op jit(solution)/shard_map/oc,pcxy->poxy/dot_general | solution.py:29
  84.4 6.0 %fusion.15 = bf16[2,64,24,256]{3,1,2,0:T(8,128)(2,1)S(1)} fusion(f32[2,24,256,64]{2,3,1,0:T(8,128)} %fusion.28, f32[2,24,256,64]{2,3,1,0:T(8,128)S(1)} %fusion.34, f32[2,24,256,64]{2,3,1,0:T(8,128)S(1)} %fusion.36, f32[2,24,256,64]{2,3,1,0:T(8,128)} %fusion.111, f32[2,24,256,64]{2,3,1,0:T(8,128)S(1)} %fusion.38, f32[2,24,256,64]{2,3,1,0:T(8,128)S(1)} %fusion.40, ...), kind=kOutput, calls=%fused_computation.27 | convolution fusion | flops 118751232 | bytes 28524544 | tf_op jit(solution)/shard_map/oc,pcxy->poxy/dot_general | solution.py:29
  91.6 2.7 %collective-permute-start.3 = (bf16[2,64,1,256]{3,1,2,0:T(8,128)(2,1)S(1)}, bf16[2,64,1,256]{3,1,2,0:T(8,128)(2,1)S(1)}, u32[]{:S(2)}, u32[]{:S(2)}) collective-permute-start(bf16[2,64,1,256]{3,1,2,0:T(8,128)(2,1)S(1)} %get-tuple-element.19), channel_id=1, source_target_pairs={{4,0},{8,4},{12,8},{0,12},{5,1},{9,5},{13,9},{1,13},{6,2},{10,6},{... | collective-permute-start | bytes 196616 | tf_op jit(solution)/shard_map/ppermute | solution.py:16
  100.4 2.3 %fusion.81 = f32[2,24,256,64]{2,3,1,0:T(8,128)} fusion(bf16[2,64,26,258]{3,1,2,0:T(8,128)(2,1)S(1)} %fusion.23, bf16[3,3,64,64]{3,2,1,0:T(8,128)(2,1)S(1)} %copy-done.1), kind=kOutput, calls=%fused_computation.91 | convolution fusion | flops 100663296 | bytes 4734976 | tf_op jit(solution)/shard_map/oc,pcxy->poxy/dot_general | solution.py:29
  102.7 2.2 %fusion.85 = f32[2,24,256,64]{2,3,1,0:T(8,128)} fusion(bf16[2,64,26,258]{3,1,2,0:T(8,128)(2,1)S(1)} %fusion.23, bf16[3,3,64,64]{3,2,1,0:T(8,128)(2,1)S(1)} %copy-done.1), kind=kOutput, calls=%fused_computation.96 | convolution fusion | flops 100663296 | bytes 4734976 | tf_op jit(solution)/shard_map/oc,pcxy->poxy/dot_general | solution.py:29
  107.1 2.2 %fusion.73 = f32[2,24,256,64]{2,3,1,0:T(8,128)} fusion(bf16[2,64,1,256]{3,1,2,0:T(8,128)(2,1)S(1)} %collective-permute-done.3, bf16[2,64,24,256]{3,1,2,0:T(8,128)(2,1)S(1)} %fusion.15, bf16[3,3,64,64]{3,2,1,0:T(8,128)(2,1)S(1)} %copy-done.1), kind=kOutput, calls=%fused_computation.83 | convolution fusion | flops 103809024 | bytes 4800512 | tf_op jit(solution)/shard_map/oc,pcxy->poxy/dot_general | solution.py:29
  109.3 5.9 %fusion.16 = bf16[2,64,24,256]{3,1,2,0:T(8,128)(2,1)S(1)} fusion(f32[2,24,256,64]{2,3,1,0:T(8,128)} %fusion.73, f32[2,24,256,64]{2,3,1,0:T(8,128)S(1)} %fusion.75, f32[2,24,256,64]{2,3,1,0:T(8,128)S(1)} %fusion.77, f32[2,24,256,64]{2,3,1,0:T(8,128)S(1)} %fusion.101, f32[2,24,256,64]{2,3,1,0:T(8,128)S(1)} %fusion.79, f32[2,24,256,64]{2,3,1,0:T(8,128)} %fusion.81, ...), kind=kOutput, calls=%fused_computation.28 | convolution fusion | flops 110886912 | bytes 28327936 | tf_op jit(solution)/shard_map/oc,pcxy->poxy/dot_general | solution.py:29
  115.9 3.3 %collective-permute-start.5 = (bf16[2,64,1,256]{3,1,2,0:T(8,128)(2,1)S(1)}, bf16[2,64,1,256]{3,1,2,0:T(8,128)(2,1)S(1)}, u32[]{:S(2)}, u32[]{:S(2)}) collective-permute-start(bf16[2,64,1,256]{3,1,2,0:T(8,128)(2,1)S(1)} %get-tuple-element.17), channel_id=1, source_target_pairs={{4,0},{8,4},{12,8},{0,12},{5,1},{9,5},{13,9},{1,13},{6,2},{10,6},{... | collective-permute-start | bytes 196616 | tf_op jit(solution)/shard_map/ppermute | solution.py:16
  123.2 2.5 %fusion.59 = f32[2,24,256,69]{2,3,1,0:T(8,128)} fusion(bf16[2,64,26,258]{3,1,2,0:T(8,128)(2,1)S(1)} %select_maximum_fusion, bf16[3,3,69,64]{2,3,1,0:T(8,128)(2,1)S(1)} %copy-done.2), kind=kOutput, calls=%fused_computation.70 | convolution fusion | flops 108527616 | bytes 4980736 | tf_op jit(solution)/shard_map/oc,pcxy->poxy/dot_general | solution.py:29
  125.7 2.6 %fusion.61 = f32[2,24,256,69]{2,3,1,0:T(8,128)} fusion(bf16[2,64,26,258]{3,1,2,0:T(8,128)(2,1)S(1)} %select_maximum_fusion, bf16[3,3,69,64]{2,3,1,0:T(8,128)(2,1)S(1)} %copy-done.2), kind=kOutput, calls=%fused_computation.72 | convolution fusion | flops 108527616 | bytes 4980736 | tf_op jit(solution)/shard_map/oc,pcxy->poxy/dot_general | solution.py:29
  128.2 2.5 %fusion.63 = f32[2,24,256,69]{2,3,1,0:T(8,128)} fusion(bf16[2,64,26,258]{3,1,2,0:T(8,128)(2,1)S(1)} %select_maximum_fusion, bf16[3,3,69,64]{2,3,1,0:T(8,128)(2,1)S(1)} %copy-done.2), kind=kOutput, calls=%fused_computation.74 | convolution fusion | flops 108527616 | bytes 4980736 | tf_op jit(solution)/shard_map/oc,pcxy->poxy/dot_general | solution.py:29
  130.8 2.5 %fusion.65 = f32[2,24,256,69]{2,3,1,0:T(8,128)} fusion(bf16[2,64,26,258]{3,1,2,0:T(8,128)(2,1)S(1)} %select_maximum_fusion, bf16[3,3,69,64]{2,3,1,0:T(8,128)(2,1)S(1)} %copy-done.2), kind=kOutput, calls=%fused_computation.76 | convolution fusion | flops 108527616 | bytes 4980736 | tf_op jit(solution)/shard_map/oc,pcxy->poxy/dot_general | solution.py:29
  133.3 2.4 %fusion.67 = f32[2,24,256,69]{2,3,1,0:T(8,128)} fusion(bf16[2,64,26,258]{3,1,2,0:T(8,128)(2,1)S(1)} %select_maximum_fusion, bf16[3,3,69,64]{2,3,1,0:T(8,128)(2,1)S(1)} %copy-done.2), kind=kOutput, calls=%fused_computation.78 | convolution fusion | flops 108527616 | bytes 4980736 | tf_op jit(solution)/shard_map/oc,pcxy->poxy/dot_general | solution.py:29
  135.7 2.4 %fusion.47 = f32[2,24,256,69]{2,3,1,0:T(8,128)} fusion(bf16[2,64,24,256]{3,1,2,0:T(8,128)(2,1)S(1)} %fusion.16, bf16[2,64,1,256]{3,1,2,0:T(8,128)(2,1)S(1)} %collective-permute-done.4, bf16[3,3,69,64]{2,3,1,0:T(8,128)(2,1)S(1)} %copy-done.2), kind=kOutput, calls=%fused_computation.60 | convolution fusion | flops 111804416 | bytes 5046272 | tf_op jit(solution)/shard_map/oc,pcxy->poxy/dot_general | solution.py:29
  138.1 2.4 %fusion.51 = f32[2,24,256,69]{2,3,1,0:T(8,128)} fusion(bf16[2,64,1,256]{3,1,2,0:T(8,128)(2,1)S(1)} %collective-permute-done.5, bf16[2,64,24,256]{3,1,2,0:T(8,128)(2,1)S(1)} %fusion.16, bf16[3,3,69,64]{2,3,1,0:T(8,128)(2,1)S(1)} %copy-done.2), kind=kOutput, calls=%fused_computation.64 | convolution fusion | flops 111804416 | bytes 5046272 | tf_op jit(solution)/shard_map/oc,pcxy->poxy/dot_general | solution.py:29
  140.5 10.1 %fusion.3 = bf16[2,69,24,256]{3,1,2,0:T(8,128)(2,1)S(1)} fusion(f32[2,24,256,69]{2,3,1,0:T(8,128)} %fusion.51, f32[2,24,256,69]{2,3,1,0:T(8,128)} %fusion.59, f32[2,24,256,69]{2,3,1,0:T(8,128)} %fusion.61, f32[2,24,256,69]{2,3,1,0:T(8,128)S(1)} %fusion.91, f32[2,24,256,69]{2,3,1,0:T(8,128)} %fusion.63, f32[2,24,256,69]{2,3,1,0:T(8,128)} %fusion.65, ...), kind=kOutput, calls=%fused_computation.11 | convolution fusion | flops 122941440 | bytes 34055168 | tf_op jit(solution)/shard_map/oc,pcxy->poxy/dot_general | solution.py:29
  (58 shorter events, 30.0 us)
Async XLA Ops:
  7.2 2.2 %copy-start = (bf16[2,69,24,256]{3,2,1,0:T(8,128)(2,1)S(1)}, bf16[2,69,24,256]{3,2,1,0:T(8,128)(2,1)}, u32[]{:S(2)}) copy-start(bf16[2,69,24,256]{3,2,1,0:T(8,128)(2,1)} %param.9) | copy-start | bytes 5087236
  7.2 2.1 %copy-start.5 = (s32[24,256]{1,0:T(8,128)S(1)}, s32[24,256]{1,0:T(8,128)}, u32[]{:S(2)}) copy-start(s32[24,256]{1,0:T(8,128)} %param.12) | copy-start | bytes 73732
  7.2 2.1 %copy-start.4 = (f32[24,256]{1,0:T(8,128)S(1)}, f32[24,256]{1,0:T(8,128)}, u32[]{:S(2)}) copy-start(f32[24,256]{1,0:T(8,128)} %param.11) | copy-start | bytes 73732
  7.2 54.4 %all-gather.2.cloned.1.call-start = ((), (), s32[]{:S(2)}) async-start(), calls=%async_computation | async-start | bytes 8478720 | tf_op jit(solution)/shard_map/all_gather | solution.py:55
  7.9 15.7 %copy-start.7 = (u32[32]{0:T(128)S(1)}, u32[32]{0:T(128)}, u32[]{:S(2)}) copy-start(u32[32]{0:T(128)} %constant.60) | copy-start | bytes 388
  7.9 28.4 %copy-start.6 = (s32[2]{0:T(128)S(1)}, s32[2]{0:T(128)}, u32[]{:S(2)}) copy-start(s32[2]{0:T(128)} %param.13) | copy-start | bytes 28
  65.2 4.4 %copy-start.3 = (bf16[3,3,64,69]{3,2,1,0:T(8,128)(2,1)S(1)}, bf16[3,3,64,69]{3,2,1,0:T(8,128)(2,1)}, u32[]{:S(2)}) copy-start(bf16[3,3,64,69]{3,2,1,0:T(8,128)(2,1)} %param.15) | copy-start | bytes 238468
  65.7 6.7 %collective-permute-start = (bf16[2,69,1,256]{3,1,2,0:T(8,128)(2,1)S(1)}, bf16[2,69,1,256]{3,1,2,0:T(8,128)(2,1)S(1)}, u32[]{:S(2)}, u32[]{:S(2)}) collective-permute-start(bf16[2,69,1,256]{3,1,2,0:T(8,128)(2,1)S(1)} %get-tuple-element.14), channel_id=1, source_target_pairs={{0,4},{4,8},{8,12},{12,0},{1,5},{5,9},{9,13},{13,1},{2,6},{6,10},{... | collective-permute-start | bytes 211976 | tf_op jit(solution)/shard_map/ppermute | solution.py:13
  67.2 5.7 %collective-permute-start.1 = (bf16[2,69,1,256]{3,1,2,0:T(8,128)(2,1)S(1)}, bf16[2,69,1,256]{3,1,2,0:T(8,128)(2,1)S(1)}, u32[]{:S(2)}, u32[]{:S(2)}) collective-permute-start(bf16[2,69,1,256]{3,1,2,0:T(8,128)(2,1)S(1)} %get-tuple-element.15), channel_id=1, source_target_pairs={{4,0},{8,4},{12,8},{0,12},{5,1},{9,5},{13,9},{1,13},{6,2},{10,6},{... | collective-permute-start | bytes 211976 | tf_op jit(solution)/shard_map/ppermute | solution.py:16
  84.4 9.9 %copy-start.1 = (bf16[3,3,64,64]{3,2,1,0:T(8,128)(2,1)S(1)}, bf16[3,3,64,64]{3,2,1,0:T(8,128)(2,1)}, u32[]{:S(2)}) copy-start(bf16[3,3,64,64]{3,2,1,0:T(8,128)(2,1)} %param.16) | copy-start | bytes 221188
  90.4 6.3 %collective-permute-start.2 = (bf16[2,64,1,256]{3,1,2,0:T(8,128)(2,1)S(1)}, bf16[2,64,1,256]{3,1,2,0:T(8,128)(2,1)S(1)}, u32[]{:S(2)}, u32[]{:S(2)}) collective-permute-start(bf16[2,64,1,256]{3,1,2,0:T(8,128)(2,1)S(1)} %get-tuple-element.18), channel_id=1, source_target_pairs={{0,4},{4,8},{8,12},{12,0},{1,5},{5,9},{9,13},{13,1},{2,6},{6,10},{... | collective-permute-start | bytes 196616 | tf_op jit(solution)/shard_map/ppermute | solution.py:13
  91.6 5.2 %collective-permute-start.3 = (bf16[2,64,1,256]{3,1,2,0:T(8,128)(2,1)S(1)}, bf16[2,64,1,256]{3,1,2,0:T(8,128)(2,1)S(1)}, u32[]{:S(2)}, u32[]{:S(2)}) collective-permute-start(bf16[2,64,1,256]{3,1,2,0:T(8,128)(2,1)S(1)} %get-tuple-element.19), channel_id=1, source_target_pairs={{4,0},{8,4},{12,8},{0,12},{5,1},{9,5},{13,9},{1,13},{6,2},{10,6},{... | collective-permute-start | bytes 196616 | tf_op jit(solution)/shard_map/ppermute | solution.py:16
  109.3 9.9 %copy-start.2 = (bf16[3,3,69,64]{2,3,1,0:T(8,128)(2,1)S(1)}, bf16[3,3,69,64]{2,3,1,0:T(8,128)(2,1)}, u32[]{:S(2)}) copy-start(bf16[3,3,69,64]{2,3,1,0:T(8,128)(2,1)} %param.17) | copy-start | bytes 238468
  115.3 6.2 %collective-permute-start.4 = (bf16[2,64,1,256]{3,1,2,0:T(8,128)(2,1)S(1)}, bf16[2,64,1,256]{3,1,2,0:T(8,128)(2,1)S(1)}, u32[]{:S(2)}, u32[]{:S(2)}) collective-permute-start(bf16[2,64,1,256]{3,1,2,0:T(8,128)(2,1)S(1)} %get-tuple-element.16), channel_id=1, source_target_pairs={{0,4},{4,8},{8,12},{12,0},{1,5},{5,9},{9,13},{13,1},{2,6},{6,10},{... | collective-permute-start | bytes 196616 | tf_op jit(solution)/shard_map/ppermute | solution.py:13
  115.9 5.6 %collective-permute-start.5 = (bf16[2,64,1,256]{3,1,2,0:T(8,128)(2,1)S(1)}, bf16[2,64,1,256]{3,1,2,0:T(8,128)(2,1)S(1)}, u32[]{:S(2)}, u32[]{:S(2)}) collective-permute-start(bf16[2,64,1,256]{3,1,2,0:T(8,128)(2,1)S(1)} %get-tuple-element.17), channel_id=1, source_target_pairs={{4,0},{8,4},{12,8},{0,12},{5,1},{9,5},{13,9},{1,13},{6,2},{10,6},{... | collective-permute-start | bytes 196616 | tf_op jit(solution)/shard_map/ppermute | solution.py:16
Sparse Core Ops, SparseCore 0:
  9.6 51.9 all-gather.1
where the time goes:
time: 159 us
  matrix products  63.2 us (40%)
  waiting for transfers between devices  30.2 us (19%)
  blocking collectives  19.6 us (12%)
  between operations  16.9 us (11%)
  starting transfers between devices  11.7 us (7%)
  other arithmetic  9.41 us (6%)
  local copies, waits for them, and re-layouts  7.92 us (5%)
    dot_general x27, matrix products, conv_local(): jnp.einsum('oc,pcxy->poxy', weight[row_tap, col_tap], window, preferred_e...  63.2 us
    all_gather x1, waiting for transfers between devices, continue_slots(): slab_piece = lax.all_gather(slabs, 'dom', axis=0, tiled=True)  25.2 us
    psum x1, blocking collectives, on_device(): band_sums = lax.psum(local_sums, 'lon')  13.4 us
    ppermute x3, starting transfers between devices, extended_2(): lax.ppermute(lax.slice_in_dim(block, 0, width, axis=dim), axis, backward)  8.36 us
    unnamed x1, blocking collectives  6.14 us
    concatenate x3, other arithmetic, extended_2(): block = jnp.concatenate([low, block, high], axis=dim)  5.59 us
    ppermute x3, waiting for transfers between devices, extended_2(): lax.ppermute(lax.slice_in_dim(block, block.shape[dim] - width, None, axis...  3.61 us
    gather x1, local copies, waits for them, and re-layouts, continue_slots(): jnp.take(slab_piece, jnp.clip(slot_ancestors, 0, piece_rows - 1), axis=0)  3.58 us
  transfers between devices with their start and end apart: 7, of which 6 were waited for; matrix products, arithmetic and copies ran while one was open for 6% of the time, Pallas kernels for 0%

commit v1 on v0

--- a/solution.py
+++ b/solution.py
@@ -52,7 +52,27 @@
 
 
 def continue_slots(slabs, slot_ancestors):
-    slab_piece = lax.all_gather(slabs, "dom", axis=0, tiled=True)
+
+    def play_sums_all(peer_axis, load):
+        axis_total = lax.psum(1, peer_axis)
+        views = []
+        for it in range(axis_total):
+            views.append((it, (it + 1) % axis_total))
+        chunks = []
+        for it in range(axis_total):
+            chunks.append((it, (it - 1) % axis_total))
+        out_arr, placed = ([load], [load])
+        for _ in range(axis_total // 2):
+            out_arr.append(lax.ppermute(out_arr[-1], peer_axis, views))
+        for _ in range((axis_total - 1) // 2):
+            placed.append(lax.ppermute(placed[-1], peer_axis, chunks))
+        return jnp.roll(
+            jnp.concatenate([*out_arr[::-1], *placed[1:]], axis=0),
+            (lax.axis_index(peer_axis) - axis_total // 2) * load.shape[0],
+            0,
+        )
+
+    slab_piece = play_sums_all("dom", slabs)
     piece_rows = slab_piece.shape[0]
     inside = (slot_ancestors >= 0) & (slot_ancestors < piece_rows)
     chosen = jnp.take(slab_piece, jnp.clip(slot_ancestors, 0, piece_rows - 1), axis=0)

time: 159 us -> 187 us (1.18)
  local copies, waits for them, and re-layouts: 7.92 us -> 33.3 us
  blocking collectives: 19.6 us -> 36.7 us
  between operations: 16.9 us -> 3.53 us
  waiting for transfers between devices: 30.2 us -> 25 us
  starting transfers between devices: 11.7 us -> 14.1 us
    all_gather x1 -> x0, waiting for transfers between devices: 25.2 us -> none  [continue_slots(): slab_piece = lax.all_gather(slabs, 'dom', axis=0, tiled=True)]
    ppermute x0 -> x3, waiting for transfers between devices: none -> 21.7 us  [the longest x2 21.7 us: play_sums_all(): out_arr.append(lax.ppermute(out_arr[-1], peer_axis, views))]
    unnamed x1, blocking collectives: 6.14 us -> 23.9 us
    unnamed x20 -> x23, local copies, waits for them, and re-layouts: 2.38 us -> 18.9 us
    dynamic_slice x0 -> x1, local copies, waits for them, and re-layouts: none -> 6.07 us  [play_sums_all(): jnp.roll(jnp.concatenate([*out_arr[::-1], *placed[1:]], axis=0), (lax.axi...]
    concatenate x0 -> x1, local copies, waits for them, and re-layouts: none -> 2.84 us  [play_sums_all(): jnp.roll(jnp.concatenate([*out_arr[::-1], *placed[1:]], axis=0), (lax.axi...]
    ppermute x0 -> x3, starting transfers between devices: none -> 2.25 us  [the longest x1 1.74 us: play_sums_all(): placed.append(lax.ppermute(placed[-1], peer_axis, chunks))]
  transfers between devices with their start and end apart: 7 -> 9, of which waited for: 6 -> 4; matrix products, arithmetic and copies ran while one was open for 6% -> 9% of each run, Pallas kernels for 0% -> 0%
where the time goes in v1:
time: 187 us; the launch traced here: 186 us
  matrix products  63.2 us (34%)
  blocking collectives  36.7 us (20%)
  local copies, waits for them, and re-layouts  33.3 us (18%)
  waiting for transfers between devices  25 us (13%)
  starting transfers between devices  14.1 us (8%)
  other arithmetic  10.2 us (5%)
  between operations  3.53 us (2%)
    dot_general x27, matrix products, conv_local(): jnp.einsum('oc,pcxy->poxy', weight[row_tap, col_tap], window, preferred_e...  63.2 us
    unnamed x1, blocking collectives  23.9 us
    ppermute x2, waiting for transfers between devices, play_sums_all(): out_arr.append(lax.ppermute(out_arr[-1], peer_axis, views))  21.7 us
    unnamed x23, local copies, waits for them, and re-layouts  18.9 us
    psum x1, blocking collectives, on_device(): band_sums = lax.psum(local_sums, 'lon')  12.8 us
    ppermute x3, starting transfers between devices, extended_2(): lax.ppermute(lax.slice_in_dim(block, 0, width, axis=dim), axis, backward)  8.15 us
    dynamic_slice x1, local copies, waits for them, and re-layouts, play_sums_all(): jnp.roll(jnp.concatenate([*out_arr[::-1], *placed[1:]], axis=0), (lax.axi...  6.07 us
    concatenate x3, other arithmetic, extended_2(): block = jnp.concatenate([low, block, high], axis=dim)  5.59 us
  transfers between devices with their start and end apart: 9, of which 4 were waited for; matrix products, arithmetic and copies ran while one was open for 9% of the time, Pallas kernels for 0%

profile of v1, /device:TPU:0, one launch (start us, length us, event | category | flops | bytes accessed | tf_op | source)
XLA Modules:
  0.0 186.0 jit_solution(8505134122628778350)
XLA Ops:
  1.1 21.7 %collective-permute-done = bf16[2,69,24,256]{3,2,1,0:T(8,128)(2,1)} collective-permute-done((bf16[2,69,24,256]{3,2,1,0:T(8,128)(2,1)}, bf16[2,69,24,256]{3,2,1,0:T(8,128)(2,1)}, u32[]{:S(2)}, u32[]{:S(2)}) %collective-permute-start) | collective-permute-done | bytes 1695776 | tf_op jit(solution)/shard_map/ppermute | solution.py:66
  27.6 12.8 %psum.7 = f32[2]{0:T(128)S(1)} all-reduce(f32[2]{0:T(128)S(1)} %fusion.5), channel_id=1, replica_groups=mesh['ens'=2,'lon'=4,'dom'=4] {'lon'}, use_global_device_ids=true, to_apply=%region_1.0 | all-reduce | flops 2 | bytes 16 | tf_op jit(solution)/shard_map/psum | solution.py:86
  41.8 23.9 %all-reduce.3 = f32[8]{0:T(128)S(1)} all-reduce(f32[8]{0:T(128)S(1)} %dynamic-update-slice), channel_id=1, replica_groups=mesh['ens'=2,'lon'=4,'dom'=4] {'dom'}, use_global_device_ids=true, to_apply=%add.3 | all-reduce | flops 8 | bytes 64
  70.9 2.7 %constant_dynamic-update-slice_fusion.7 = bf16[16,69,24,256]{3,2,1,0:T(8,128)(2,1)} fusion(bf16[2,69,24,256]{3,2,1,0:T(8,128)(2,1)} %collective-permute-done.1), kind=kLoop, calls=%fused_computation.106 | loop fusion | bytes 3391488
  73.6 2.7 %constant_dynamic-update-slice_fusion.6 = bf16[16,69,24,256]{3,2,1,0:T(8,128)(2,1)} fusion(bf16[16,69,24,256]{3,2,1,0:T(8,128)(2,1)} %constant_dynamic-update-slice_fusion.7, bf16[2,69,24,256]{3,2,1,0:T(8,128)(2,1)} %collective-permute-done), kind=kLoop, calls=%fused_computation.105 | loop fusion | bytes 3391488
  77.7 2.8 %constant_dynamic-update-slice_fusion.4 = bf16[16,69,24,256]{3,2,1,0:T(8,128)(2,1)} fusion(bf16[16,69,24,256]{3,2,1,0:T(8,128)(2,1)} %constant_dynamic-update-slice_fusion.5, bf16[2,69,24,256]{3,2,1,0:T(8,128)(2,1)} %collective-permute-done.2), kind=kLoop, calls=%fused_computation.103 | loop fusion | bytes 3391488
  80.5 2.8 %constant_dynamic-update-slice_fusion.3 = bf16[16,69,24,256]{3,2,1,0:T(8,128)(2,1)} fusion(bf16[16,69,24,256]{3,2,1,0:T(8,128)(2,1)} %constant_dynamic-update-slice_fusion.4, bf16[2,69,24,256]{3,2,1,0:T(8,128)(2,1)} %collective-permute-done.1), kind=kLoop, calls=%fused_computation.102 | loop fusion | bytes 3391488
  83.3 2.8 %constant_dynamic-update-slice_fusion.2 = bf16[16,69,24,256]{3,2,1,0:T(8,128)(2,1)} fusion(bf16[16,69,24,256]{3,2,1,0:T(8,128)(2,1)} %constant_dynamic-update-slice_fusion.3, bf16[2,69,24,256]{3,2,1,0:T(8,128)(2,1)} %collective-permute-done), kind=kLoop, calls=%fused_computation.101 | loop fusion | bytes 3391488
  87.4 2.8 %constant_dynamic-update-slice_fusion = bf16[16,69,24,256]{3,2,1,0:T(8,128)(2,1)} fusion(bf16[16,69,24,256]{3,2,1,0:T(8,128)(2,1)} %constant_dynamic-update-slice_fusion.1, bf16[2,69,24,256]{3,2,1,0:T(8,128)(2,1)} %collective-permute-done.2), kind=kLoop, calls=%fused_computation.99 | loop fusion | bytes 3391488 | tf_op jit(solution)/shard_map/jit(_roll_dynamic)/concatenate | solution.py:69
  90.2 6.1 %constant_dynamic-slice_fusion = bf16[8,69,24,256]{3,2,1,0:T(8,128)(2,1)} fusion(bf16[16,69,24,256]{3,2,1,0:T(8,128)(2,1)} %constant_dynamic-update-slice_fusion, s32[]{:T(128)S(6)} %select_n.31), kind=kLoop, calls=%fused_computation.172 | loop fusion | bytes 13565956 | tf_op jit(solution)/shard_map/jit(_roll_dynamic)/dynamic_slice | solution.py:69
  96.3 3.6 %gather_fusion = bf16[2,69,24,256]{3,2,1,0:T(8,128)(2,1)S(1)} fusion(bf16[8,69,24,256]{3,2,1,0:T(8,128)(2,1)} %constant_dynamic-slice_fusion, s32[1024]{0:T(1024)S(1)} %pad_clamp_fusion), kind=kCustom, calls=%fused_computation | custom fusion | bytes 3391496 | tf_op jit(solution)/shard_map/jit(_take)/gather | solution.py:78
  101.8 2.5 %collective-permute-start.4 = (bf16[2,69,1,256]{3,1,2,0:T(8,128)(2,1)S(1)}, bf16[2,69,1,256]{3,1,2,0:T(8,128)(2,1)S(1)}, u32[]{:S(2)}, u32[]{:S(2)}) collective-permute-start(bf16[2,69,1,256]{3,1,2,0:T(8,128)(2,1)S(1)} %get-tuple-element.13), channel_id=1, source_target_pairs={{4,0},{8,4},{12,8},{0,12},{5,1},{9,5},{13,9},{1,13},{6,2},{10,6},{... | collective-permute-start | bytes 211976 | tf_op jit(solution)/shard_map/ppermute | solution.py:16
  104.2 2.6 %fusion.111 = f32[2,24,256,64]{2,3,1,0:T(8,128)} fusion(bf16[3,3,64,69]{3,2,1,0:T(8,128)(2,1)S(1)} %copy-done.3, bf16[2,69,24,256]{3,2,1,0:T(8,128)(2,1)S(1)} %gather_fusion, pred[2]{0:T(512)(128)(4,1)S(1)} %get-tuple-element.10, pred[2]{0:T(512)(128)(4,1)S(1)} %get-tuple-element.18), kind=kOutput, calls=%fused_computation.131 | convolution fusion | flops 110223360 | bytes 4858880 | tf_op jit(solution)/shard_map/oc,pcxy->poxy/dot_general | solution.py:29
  118.4 6.0 %fusion.15 = bf16[2,64,24,256]{3,1,2,0:T(8,128)(2,1)S(1)} fusion(f32[2,24,256,64]{2,3,1,0:T(8,128)} %fusion.28, f32[2,24,256,64]{2,3,1,0:T(8,128)S(1)} %fusion.34, f32[2,24,256,64]{2,3,1,0:T(8,128)S(1)} %fusion.36, f32[2,24,256,64]{2,3,1,0:T(8,128)} %fusion.111, f32[2,24,256,64]{2,3,1,0:T(8,128)S(1)} %fusion.38, f32[2,24,256,64]{2,3,1,0:T(8,128)S(1)} %fusion.40, ...), kind=kOutput, calls=%fused_computation.27 | convolution fusion | flops 118751232 | bytes 28524544 | tf_op jit(solution)/shard_map/oc,pcxy->poxy/dot_general | solution.py:29
  125.5 2.8 %collective-permute-start.6 = (bf16[2,64,1,256]{3,1,2,0:T(8,128)(2,1)S(1)}, bf16[2,64,1,256]{3,1,2,0:T(8,128)(2,1)S(1)}, u32[]{:S(2)}, u32[]{:S(2)}) collective-permute-start(bf16[2,64,1,256]{3,1,2,0:T(8,128)(2,1)S(1)} %get-tuple-element.17), channel_id=1, source_target_pairs={{4,0},{8,4},{12,8},{0,12},{5,1},{9,5},{13,9},{1,13},{6,2},{10,6},{... | collective-permute-start | bytes 196616 | tf_op jit(solution)/shard_map/ppermute | solution.py:16
  143.1 5.9 %fusion.16 = bf16[2,64,24,256]{3,1,2,0:T(8,128)(2,1)S(1)} fusion(f32[2,24,256,64]{2,3,1,0:T(8,128)} %fusion.73, f32[2,24,256,64]{2,3,1,0:T(8,128)S(1)} %fusion.75, f32[2,24,256,64]{2,3,1,0:T(8,128)S(1)} %fusion.77, f32[2,24,256,64]{2,3,1,0:T(8,128)S(1)} %fusion.101, f32[2,24,256,64]{2,3,1,0:T(8,128)S(1)} %fusion.79, f32[2,24,256,64]{2,3,1,0:T(8,128)} %fusion.81, ...), kind=kOutput, calls=%fused_computation.28 | convolution fusion | flops 110886912 | bytes 28327936 | tf_op jit(solution)/shard_map/oc,pcxy->poxy/dot_general | solution.py:29
  150.3 2.9 %collective-permute-start.8 = (bf16[2,64,1,256]{3,1,2,0:T(8,128)(2,1)S(1)}, bf16[2,64,1,256]{3,1,2,0:T(8,128)(2,1)S(1)}, u32[]{:S(2)}, u32[]{:S(2)}) collective-permute-start(bf16[2,64,1,256]{3,1,2,0:T(8,128)(2,1)S(1)} %get-tuple-element.15), channel_id=1, source_target_pairs={{4,0},{8,4},{12,8},{0,12},{5,1},{9,5},{13,9},{1,13},{6,2},{10,6},{... | collective-permute-start | bytes 196616 | tf_op jit(solution)/shard_map/ppermute | solution.py:16
  157.1 2.5 %fusion.59 = f32[2,24,256,69]{2,3,1,0:T(8,128)} fusion(bf16[2,64,26,258]{3,1,2,0:T(8,128)(2,1)S(1)} %select_maximum_fusion, bf16[3,3,69,64]{2,3,1,0:T(8,128)(2,1)S(1)} %copy-done.2), kind=kOutput, calls=%fused_computation.70 | convolution fusion | flops 108527616 | bytes 4980736 | tf_op jit(solution)/shard_map/oc,pcxy->poxy/dot_general | solution.py:29
  159.5 2.6 %fusion.61 = f32[2,24,256,69]{2,3,1,0:T(8,128)} fusion(bf16[2,64,26,258]{3,1,2,0:T(8,128)(2,1)S(1)} %select_maximum_fusion, bf16[3,3,69,64]{2,3,1,0:T(8,128)(2,1)S(1)} %copy-done.2), kind=kOutput, calls=%fused_computation.72 | convolution fusion | flops 108527616 | bytes 4980736 | tf_op jit(solution)/shard_map/oc,pcxy->poxy/dot_general | solution.py:29
  162.1 2.5 %fusion.63 = f32[2,24,256,69]{2,3,1,0:T(8,128)} fusion(bf16[2,64,26,258]{3,1,2,0:T(8,128)(2,1)S(1)} %select_maximum_fusion, bf16[3,3,69,64]{2,3,1,0:T(8,128)(2,1)S(1)} %copy-done.2), kind=kOutput, calls=%fused_computation.74 | convolution fusion | flops 108527616 | bytes 4980736 | tf_op jit(solution)/shard_map/oc,pcxy->poxy/dot_general | solution.py:29
  164.7 2.5 %fusion.65 = f32[2,24,256,69]{2,3,1,0:T(8,128)} fusion(bf16[2,64,26,258]{3,1,2,0:T(8,128)(2,1)S(1)} %select_maximum_fusion, bf16[3,3,69,64]{2,3,1,0:T(8,128)(2,1)S(1)} %copy-done.2), kind=kOutput, calls=%fused_computation.76 | convolution fusion | flops 108527616 | bytes 4980736 | tf_op jit(solution)/shard_map/oc,pcxy->poxy/dot_general | solution.py:29
  167.1 2.4 %fusion.67 = f32[2,24,256,69]{2,3,1,0:T(8,128)} fusion(bf16[2,64,26,258]{3,1,2,0:T(8,128)(2,1)S(1)} %select_maximum_fusion, bf16[3,3,69,64]{2,3,1,0:T(8,128)(2,1)S(1)} %copy-done.2), kind=kOutput, calls=%fused_computation.78 | convolution fusion | flops 108527616 | bytes 4980736 | tf_op jit(solution)/shard_map/oc,pcxy->poxy/dot_general | solution.py:29
  169.5 2.4 %fusion.47 = f32[2,24,256,69]{2,3,1,0:T(8,128)} fusion(bf16[2,64,24,256]{3,1,2,0:T(8,128)(2,1)S(1)} %fusion.16, bf16[2,64,1,256]{3,1,2,0:T(8,128)(2,1)S(1)} %collective-permute-done.7, bf16[3,3,69,64]{2,3,1,0:T(8,128)(2,1)S(1)} %copy-done.2), kind=kOutput, calls=%fused_computation.60 | convolution fusion | flops 111804416 | bytes 5046272 | tf_op jit(solution)/shard_map/oc,pcxy->poxy/dot_general | solution.py:29
  174.4 10.1 %fusion.3 = bf16[2,69,24,256]{3,1,2,0:T(8,128)(2,1)S(1)} fusion(f32[2,24,256,69]{2,3,1,0:T(8,128)} %fusion.51, f32[2,24,256,69]{2,3,1,0:T(8,128)} %fusion.59, f32[2,24,256,69]{2,3,1,0:T(8,128)} %fusion.61, f32[2,24,256,69]{2,3,1,0:T(8,128)S(1)} %fusion.91, f32[2,24,256,69]{2,3,1,0:T(8,128)} %fusion.63, f32[2,24,256,69]{2,3,1,0:T(8,128)} %fusion.65, ...), kind=kOutput, calls=%fused_computation.11 | convolution fusion | flops 122941440 | bytes 34055168 | tf_op jit(solution)/shard_map/oc,pcxy->poxy/dot_general | solution.py:29
  (66 shorter events, 50.1 us)
Async XLA Ops:
  0.6 26.1 %copy-start = (bf16[2,69,24,256]{3,2,1,0:T(8,128)(2,1)S(1)}, bf16[2,69,24,256]{3,2,1,0:T(8,128)(2,1)}, u32[]{:S(2)}) copy-start(bf16[2,69,24,256]{3,2,1,0:T(8,128)(2,1)} %param.9) | copy-start | bytes 5087236
  0.6 22.2 %collective-permute-start = (bf16[2,69,24,256]{3,2,1,0:T(8,128)(2,1)}, bf16[2,69,24,256]{3,2,1,0:T(8,128)(2,1)}, u32[]{:S(2)}, u32[]{:S(2)}) collective-permute-start(bf16[2,69,24,256]{3,2,1,0:T(8,128)(2,1)} %param.9), channel_id=1, source_target_pairs={{0,1},{1,2},{2,3},{3,0},{4,5},{5,6},{6,7},{7,4},{8,9},{9,10},{10,1... | collective-permute-start | bytes 5087240 | tf_op jit(solution)/shard_map/ppermute | solution.py:66
  22.8 48.0 %collective-permute-start.1 = (bf16[2,69,24,256]{3,2,1,0:T(8,128)(2,1)}, bf16[2,69,24,256]{3,2,1,0:T(8,128)(2,1)}, u32[]{:S(2)}, u32[]{:S(2)}) collective-permute-start(bf16[2,69,24,256]{3,2,1,0:T(8,128)(2,1)} %collective-permute-done), channel_id=1, source_target_pairs={{0,1},{1,2},{2,3},{3,0},{4,5},{5,6},{6,7},{7,4},{8,9},{9,10},{10,1... | collective-permute-start | bytes 5087240 | tf_op jit(solution)/shard_map/ppermute | solution.py:66
  22.8 54.9 %collective-permute-start.2 = (bf16[2,69,24,256]{3,2,1,0:T(8,128)(2,1)}, bf16[2,69,24,256]{3,2,1,0:T(8,128)(2,1)}, u32[]{:S(2)}, u32[]{:S(2)}) collective-permute-start(bf16[2,69,24,256]{3,2,1,0:T(8,128)(2,1)} %param.9), channel_id=1, source_target_pairs={{0,3},{1,0},{2,1},{3,2},{4,7},{5,4},{6,5},{7,6},{8,11},{9,8},{10,9... | collective-permute-start | bytes 5087240 | tf_op jit(solution)/shard_map/ppermute | solution.py:68
  25.3 15.0 %copy-start.5 = (u32[32]{0:T(128)S(1)}, u32[32]{0:T(128)}, u32[]{:S(2)}) copy-start(u32[32]{0:T(128)} %constant.81) | copy-start | bytes 388
  25.3 45.5 %copy-start.4 = (s32[2]{0:T(128)S(1)}, s32[2]{0:T(128)}, u32[]{:S(2)}) copy-start(s32[2]{0:T(128)} %param.13) | copy-start | bytes 28
  99.9 4.4 %copy-start.3 = (bf16[3,3,64,69]{3,2,1,0:T(8,128)(2,1)S(1)}, bf16[3,3,64,69]{3,2,1,0:T(8,128)(2,1)}, u32[]{:S(2)}) copy-start(bf16[3,3,64,69]{3,2,1,0:T(8,128)(2,1)} %param.15) | copy-start | bytes 238468
  100.4 6.5 %collective-permute-start.3 = (bf16[2,69,1,256]{3,1,2,0:T(8,128)(2,1)S(1)}, bf16[2,69,1,256]{3,1,2,0:T(8,128)(2,1)S(1)}, u32[]{:S(2)}, u32[]{:S(2)}) collective-permute-start(bf16[2,69,1,256]{3,1,2,0:T(8,128)(2,1)S(1)} %get-tuple-element.12), channel_id=1, source_target_pairs={{0,4},{4,8},{8,12},{12,0},{1,5},{5,9},{9,13},{13,1},{2,6},{6,10},{... | collective-permute-start | bytes 211976 | tf_op jit(solution)/shard_map/ppermute | solution.py:13
  101.8 5.1 %collective-permute-start.4 = (bf16[2,69,1,256]{3,1,2,0:T(8,128)(2,1)S(1)}, bf16[2,69,1,256]{3,1,2,0:T(8,128)(2,1)S(1)}, u32[]{:S(2)}, u32[]{:S(2)}) collective-permute-start(bf16[2,69,1,256]{3,1,2,0:T(8,128)(2,1)S(1)} %get-tuple-element.13), channel_id=1, source_target_pairs={{4,0},{8,4},{12,8},{0,12},{5,1},{9,5},{13,9},{1,13},{6,2},{10,6},{... | collective-permute-start | bytes 211976 | tf_op jit(solution)/shard_map/ppermute | solution.py:16
  118.4 9.9 %copy-start.1 = (bf16[3,3,64,64]{3,2,1,0:T(8,128)(2,1)S(1)}, bf16[3,3,64,64]{3,2,1,0:T(8,128)(2,1)}, u32[]{:S(2)}) copy-start(bf16[3,3,64,64]{3,2,1,0:T(8,128)(2,1)} %param.16) | copy-start | bytes 221188
  124.4 6.2 %collective-permute-start.5 = (bf16[2,64,1,256]{3,1,2,0:T(8,128)(2,1)S(1)}, bf16[2,64,1,256]{3,1,2,0:T(8,128)(2,1)S(1)}, u32[]{:S(2)}, u32[]{:S(2)}) collective-permute-start(bf16[2,64,1,256]{3,1,2,0:T(8,128)(2,1)S(1)} %get-tuple-element.16), channel_id=1, source_target_pairs={{0,4},{4,8},{8,12},{12,0},{1,5},{5,9},{9,13},{13,1},{2,6},{6,10},{... | collective-permute-start | bytes 196616 | tf_op jit(solution)/shard_map/ppermute | solution.py:13
  125.5 5.1 %collective-permute-start.6 = (bf16[2,64,1,256]{3,1,2,0:T(8,128)(2,1)S(1)}, bf16[2,64,1,256]{3,1,2,0:T(8,128)(2,1)S(1)}, u32[]{:S(2)}, u32[]{:S(2)}) collective-permute-start(bf16[2,64,1,256]{3,1,2,0:T(8,128)(2,1)S(1)} %get-tuple-element.17), channel_id=1, source_target_pairs={{4,0},{8,4},{12,8},{0,12},{5,1},{9,5},{13,9},{1,13},{6,2},{10,6},{... | collective-permute-start | bytes 196616 | tf_op jit(solution)/shard_map/ppermute | solution.py:16
  143.1 10.0 %copy-start.2 = (bf16[3,3,69,64]{2,3,1,0:T(8,128)(2,1)S(1)}, bf16[3,3,69,64]{2,3,1,0:T(8,128)(2,1)}, u32[]{:S(2)}) copy-start(bf16[3,3,69,64]{2,3,1,0:T(8,128)(2,1)} %param.17) | copy-start | bytes 238468
  149.0 6.2 %collective-permute-start.7 = (bf16[2,64,1,256]{3,1,2,0:T(8,128)(2,1)S(1)}, bf16[2,64,1,256]{3,1,2,0:T(8,128)(2,1)S(1)}, u32[]{:S(2)}, u32[]{:S(2)}) collective-permute-start(bf16[2,64,1,256]{3,1,2,0:T(8,128)(2,1)S(1)} %get-tuple-element.14), channel_id=1, source_target_pairs={{0,4},{4,8},{8,12},{12,0},{1,5},{5,9},{9,13},{13,1},{2,6},{6,10},{... | collective-permute-start | bytes 196616 | tf_op jit(solution)/shard_map/ppermute | solution.py:13
  150.3 5.0 %collective-permute-start.8 = (bf16[2,64,1,256]{3,1,2,0:T(8,128)(2,1)S(1)}, bf16[2,64,1,256]{3,1,2,0:T(8,128)(2,1)S(1)}, u32[]{:S(2)}, u32[]{:S(2)}) collective-permute-start(bf16[2,64,1,256]{3,1,2,0:T(8,128)(2,1)S(1)} %get-tuple-element.15), channel_id=1, source_target_pairs={{4,0},{8,4},{12,8},{0,12},{5,1},{9,5},{13,9},{1,13},{6,2},{10,6},{... | collective-permute-start | bytes 196616 | tf_op jit(solution)/shard_map/ppermute | solution.py:16
